TPU v7x, 256 devices: a whole 4x4x8 slice. The times are simulated.
256 devices in a mesh: ref: 64 (over z, y_lo, x), win: 4 (over y_hi, core).
Axes of the slice: x: 4, y: 4 (y_hi: 2, y_lo: 2; y = y_hi * 2 + y_lo), z: 8, core: 2. Of those that a mesh axis runs over, the one named last changes fastest.
Arguments:
- queries: bfloat16 [2048, 8192], P('ref', 'win'), may hold values from -1 to 1, as said below
- references: bfloat16 [65536, 8192], P('ref', 'win'), may hold values from -1 to 1, as said below
- labels: int32 [512], P('ref'), may hold values from 0 to 7, as said below
- kernel: float32 [9, 8], replicated, may hold values from 0.02 to 0.3
- class_bias: float32 [8], replicated, may hold values from -4 to 4
Outputs:
- ancestry_logprob: float32 [16, 8, 2048], P('win', None, 'ref')
Inputs may be any that keep to these rules, and one draw needn't show every extreme that they name: `queries`: every entry is -1 or +1. `references`: every entry is -1 or +1. Every ancestry labels at least one block.
All inputs are finite; a program needn't handle non-finite values.
Results may differ from a plain program's by a relative error of at most 0.0003.
Values may be sent and summed in bfloat16 or wider, within the bound.
A program may use at most 64 MiB of HBM per device.

v0:
```python
import jax
import jax.numpy as jnp
from jax import lax
from jax.sharding import PartitionSpec as P

S = 512
A = 8
BLOCK = 128
TAPS = 9
neg_floor = -1e30


def combined_all(shard, axis, combine):
    everything = lax.all_gather(shard, axis)
    leading = everything[0]

    def lap(k, so_far):
        return combine(so_far, everything[k])

    return lax.fori_loop(1, lax.axis_size(axis), lap, leading)


def with_halo(block, sides, width):
    for axis, dim in sides:
        count = lax.axis_size(axis)
        forward = [(i, i + 1) for i in range(count - 1)]
        backward = [(target, source) for source, target in forward]
        low = lax.ppermute(
            lax.slice_in_dim(block, block.shape[dim] - width, None, axis=dim), axis, forward
        )
        high = lax.ppermute(lax.slice_in_dim(block, 0, width, axis=dim), axis, backward)
        block = jnp.concatenate([low, block, high], axis=dim)
    return block


def pool_rows(query_piece, references, member, windows):
    score_scale = 256.0 / S
    row_count = query_piece.shape[0]
    block_count = references.shape[0] // BLOCK
    results = []
    for window in range(windows):
        query_part = query_piece[:, window * S : (window + 1) * S]
        ref_part = references[:, window * S : (window + 1) * S]
        scores = (
            jnp.einsum("qs,rs->qr", query_part, ref_part, preferred_element_type=jnp.float32)
            * score_scale
        )
        blocks = scores.reshape(row_count, block_count, BLOCK)
        block_peak = jnp.max(blocks, axis=2)
        block_total = jnp.sum(jnp.exp(blocks - block_peak[:, :, None]), axis=2)
        group_peak = jnp.max(jnp.where(member[None], block_peak[:, :, None], neg_floor), axis=1)
        weights = jnp.where(
            member[None],
            block_total[:, :, None] * jnp.exp(block_peak[:, :, None] - group_peak[:, None, :]),
            0.0,
        )
        group_total = jnp.sum(weights, axis=1)
        group_lse = jnp.where(group_total > 0, group_peak + jnp.log(group_total), neg_floor)
        results.append(group_lse.T)
    return jnp.stack(results)


def combine_lse(left_part, right_part):
    higher = jnp.maximum(left_part, right_part)
    return higher + jnp.log(jnp.exp(left_part - higher) + jnp.exp(right_part - higher))


def per_device(queries, references, labels, kernel, class_bias):
    member = labels[:, None] == jnp.arange(A, dtype=jnp.int32)[None, :]
    windows = references.shape[1] // S
    query_count = queries.shape[0]
    partial_value = pool_rows(
        lax.all_gather(queries, "ref", axis=0, tiled=True), references, member, windows
    )
    owner_start = lax.axis_index("ref") * query_count
    combined = combined_all(partial_value, "ref", combine_lse)
    pooled = lax.dynamic_slice_in_dim(combined, owner_start, query_count, 2)
    centered = pooled - jnp.mean(pooled, axis=1, keepdims=True)
    padded = with_halo(centered, (("win", 0),), TAPS // 2)
    smoothed = jnp.zeros_like(centered)
    for offset in range(TAPS):
        smoothed = smoothed + kernel[offset][None, :, None] * padded[offset : offset + windows]
    logits = smoothed + class_bias[None, :, None]
    return jax.nn.log_softmax(logits, axis=1)


def solution(mesh):
    in_specs = (P("ref", "win"), P("ref", "win"), P("ref"), P(), P())
    out_specs = P("win", None, "ref")
    return jax.shard_map(
        per_device, mesh=mesh, in_specs=in_specs, out_specs=out_specs, check_vma=False
    )
```

profile of v0, /device:TPU:1, one launch (start us, length us, event | category | flops | bytes accessed | tf_op | source)
XLA Modules:
  0.0 761.7 jit_solution(14383319232930999667)
XLA Ops:
  8.0 274.8 %all-gather.4.cloned.1.call-done = bf16[2048,2048]{1,0:T(8,128)(2,1)} async-done(((bf16[32,2048]{1,0:T(8,128)(2,1)}), bf16[2048,2048]{1,0:T(8,128)(2,1)}) %all-gather.4.cloned.1.call-update) | async-done | bytes 8388624 | tf_op jit(solution)/shard_map/all_gather | solution.py:73
  282.9 4.4 bitcast_reduce_fusion.3
  287.3 1.5 fusion.15
  288.9 1.8 copy-done.1
  290.7 2.4 bitcast_reduce_fusion
  293.1 1.5 fusion.9
  294.6 2.4 bitcast_reduce_fusion.1
  297.0 1.5 fusion.11
  298.5 2.6 bitcast_reduce_fusion.2
  301.1 1.5 fusion.13
  304.1 325.6 %all-gather.6.cloned.1.call-done = f32[256,8,2048]{2,1,0:T(8,128)} async-done(((f32[4,8,2048]{2,1,0:T(8,128)}), f32[256,8,2048]{2,1,0:T(8,128)}) %all-gather.6.cloned.1.call-update) | async-done | bytes 16777232 | tf_op jit(solution)/shard_map/all_gather | solution.py:14
  630.6 76.0 %while.15 = (s32[]{:T(128)}, f32[4,8,2048]{2,1,0:T(8,128)S(1)}, f32[64,4,8,2048]{3,2,1,0:T(8,128)}, s32[]{:T(128)}, s32[]{:T(128)}, /*index=5*/s32[]{:T(128)}) while((s32[]{:T(128)}, f32[4,8,2048]{2,1,0:T(8,128)S(1)}, f32[64,4,8,2048]{3,2,1,0:T(8,128)}, s32[]{:T(128)}, s32[]{:T(128)}, /*index=5*/s32[]{:T(128)}) %tuple.62), condition=%wide.region_17.18_spmd, body=%wide.region_16.17_spmd.sunk | while | flops 327685 | bytes 786539 | solution.py:20
  630.6 1.2 fusion.53
  631.8 1.2 fusion.53
  633.0 1.2 fusion.53
  634.2 1.2 fusion.53
  635.4 1.2 fusion.53
  636.6 1.2 fusion.53
  637.8 1.2 fusion.53
  639.0 1.2 fusion.53
  640.2 1.2 fusion.53
  641.4 1.2 fusion.53
  642.7 1.2 fusion.53
  643.9 1.2 fusion.53
  645.1 1.2 fusion.53
  646.3 1.2 fusion.53
  647.5 1.2 fusion.53
  648.7 1.2 fusion.53
  649.9 1.2 fusion.53
  651.1 1.2 fusion.53
  652.3 1.2 fusion.53
  653.5 1.2 fusion.53
  654.7 1.2 fusion.53
  655.9 1.2 fusion.53
  657.1 1.2 fusion.53
  658.3 1.2 fusion.53
  659.5 1.2 fusion.53
  660.7 1.2 fusion.53
  661.9 1.2 fusion.53
  663.2 1.2 fusion.53
  664.4 1.2 fusion.53
  665.6 1.2 fusion.53
  666.8 1.2 fusion.53
  668.0 1.2 fusion.53
  669.2 1.2 fusion.53
  670.4 1.2 fusion.53
  671.6 1.2 fusion.53
  672.8 1.2 fusion.53
  674.0 1.2 fusion.53
  675.2 1.2 fusion.53
  676.4 1.2 fusion.53
  678.8 1.2 fusion.53
  681.2 1.2 fusion.53
  683.6 1.2 fusion.53
  686.1 1.2 fusion.53
  688.5 1.2 fusion.53
  690.9 1.2 fusion.53
  693.3 1.2 fusion.53
  695.7 1.2 fusion.53
  699.3 1.2 fusion.53
  701.7 1.2 fusion.53
  704.1 1.2 fusion.53
  706.7 42.3 %collective-permute-start.1 = (f32[4,8,32]{2,1,0:T(8,128)S(1)}, f32[4,8,32]{2,1,0:T(8,128)S(1)}, u32[]{:S(2)}, u32[]{:S(2)}) collective-permute-start(f32[4,8,32]{2,1,0:T(8,128)S(1)} %dynamic-slice_subtract_fusion), channel_id=1, source_target_pairs={{1,0},{2,1},{3,2},{5,4},{6,5},{7,6},{9,8},{10,9},{11,10},{13,12},{... | collective-permute-start | bytes 12296 | tf_op jit(solution)/shard_map/ppermute | solution.py:31
  749.0 4.3 collective-permute-start
  (40 shorter events, 21.2 us)
Async XLA Ops:
  6.5 276.3 %all-gather.4.cloned.1.call-start = ((), (), s32[]{:S(2)}) async-start(), calls=%async_computation | async-start | bytes 8519680 | tf_op jit(solution)/shard_map/all_gather | solution.py:73
  7.3 622.4 %all-gather.6.cloned.1.call-start = ((), (), s32[]{:S(2)}) async-start(), calls=%async_computation.1 | async-start | bytes 17039360 | tf_op jit(solution)/shard_map/all_gather | solution.py:14
  282.9 6.0 copy-start.2
  287.3 3.4 copy-start.1
  301.1 452.2 %copy-start = (f32[9,8]{0,1:T(8,128)S(1)}, f32[9,8]{0,1:T(8,128)}, u32[]{:S(2)}) copy-start(f32[9,8]{0,1:T(8,128)} %param.10) | copy-start | bytes 868
  301.1 453.1 %copy-start.3 = (f32[8]{0:T(128)S(1)}, f32[8]{0:T(128)}, u32[]{:S(2)}) copy-start(f32[8]{0:T(128)} %param.11) | copy-start | bytes 100
  706.7 46.9 %collective-permute-start.1 = (f32[4,8,32]{2,1,0:T(8,128)S(1)}, f32[4,8,32]{2,1,0:T(8,128)S(1)}, u32[]{:S(2)}, u32[]{:S(2)}) collective-permute-start(f32[4,8,32]{2,1,0:T(8,128)S(1)} %dynamic-slice_subtract_fusion), channel_id=1, source_target_pairs={{1,0},{2,1},{3,2},{5,4},{6,5},{7,6},{9,8},{10,9},{11,10},{13,12},{... | collective-permute-start | bytes 12296 | tf_op jit(solution)/shard_map/ppermute | solution.py:31
  749.0 5.2 collective-permute-start
Sparse Core Ops, SparseCore 0:
  9.1 273.7 all-gather.3
  304.2 325.3 all-gather.5
where the time goes:
time: 764 us; the launch traced here: 762 us
  waiting for transfers between devices  602 us (79%)
  other arithmetic  83.8 us (11%)
  starting transfers between devices  46.6 us (6%)
  between operations  13.6 us (2%)
  matrix products  11.8 us (2%)
    all_gather x1, waiting for transfers between devices, combined_all(): everything = lax.all_gather(shard, axis)  326 us
    all_gather x1, waiting for transfers between devices, per_device(): lax.all_gather(queries, 'ref', axis=0, tiled=True)  275 us
    add x63, other arithmetic, combine_lse(): higher + jnp.log(jnp.exp(left_part - higher) + jnp.exp(right_part - higher))  74.7 us
    ppermute x1, starting transfers between devices, with_halo(): lax.ppermute(lax.slice_in_dim(block, 0, width, axis=dim), axis, backward)  42.3 us
  transfers between devices with their start and end apart: 4, of which 3 were waited for; matrix products, arithmetic and copies ran while one was open for 0% of the time, Pallas kernels for 0%

commit v1 on v0

--- a/solution.py
+++ b/solution.py
@@ -70,7 +70,12 @@
     windows = references.shape[1] // S
     query_count = queries.shape[0]
     partial_value = pool_rows(
-        lax.all_gather(queries, "ref", axis=0, tiled=True), references, member, windows
+        jnp.concatenate(
+            lax.all_to_all(jnp.stack([queries] * lax.axis_size("ref")), "ref", 0, 0), axis=0
+        ),
+        references,
+        member,
+        windows,
     )
     owner_start = lax.axis_index("ref") * query_count
     combined = combined_all(partial_value, "ref", combine_lse)

time: 764 us -> 661 us (0.87)
  waiting for transfers between devices: 602 us -> 471 us
  starting transfers between devices: 46.6 us -> 60.5 us
  matrix products: 11.8 us -> 19.6 us
    all_gather x1 -> x0, waiting for transfers between devices: 275 us -> none  [per_device(): lax.all_gather(queries, 'ref', axis=0, tiled=True)]
    all_to_all x0 -> x1, waiting for transfers between devices: none -> 181 us  [per_device(): lax.all_to_all(jnp.stack([queries] * lax.axis_size('ref')), 'ref', 0, 0)]
    all_gather x1, waiting for transfers between devices: 326 us -> 289 us  [combined_all(): everything = lax.all_gather(shard, axis)]
    all_to_all x0 -> x1, starting transfers between devices: none -> 13.9 us  [per_device(): lax.all_to_all(jnp.stack([queries] * lax.axis_size('ref')), 'ref', 0, 0)]
    dot_general x4, matrix products: 11.8 us -> 19.6 us  [pool_rows(): jnp.einsum('qs,rs->qr', query_part, ref_part, preferred_element_type=jnp....]
where the time goes in v1:
time: 661 us; the launch traced here: 659 us
  waiting for transfers between devices  471 us (71%)
  other arithmetic  86.7 us (13%)
  starting transfers between devices  60.5 us (9%)
  matrix products  19.6 us (3%)
  between operations  13.6 us (2%)
    all_gather x1, waiting for transfers between devices, combined_all(): everything = lax.all_gather(shard, axis)  289 us
    all_to_all x1, waiting for transfers between devices, per_device(): lax.all_to_all(jnp.stack([queries] * lax.axis_size('ref')), 'ref', 0, 0)  181 us
    add x63, other arithmetic, combine_lse(): higher + jnp.log(jnp.exp(left_part - higher) + jnp.exp(right_part - higher))  74.7 us
    ppermute x1, starting transfers between devices, with_halo(): lax.ppermute(lax.slice_in_dim(block, 0, width, axis=dim), axis, backward)  42.3 us
    dot_general x4, matrix products, pool_rows(): jnp.einsum('qs,rs->qr', query_part, ref_part, preferred_element_type=jnp....  19.6 us
    all_to_all x1, starting transfers between devices, per_device(): lax.all_to_all(jnp.stack([queries] * lax.axis_size('ref')), 'ref', 0, 0)  13.9 us
  transfers between devices with their start and end apart: 4, of which 3 were waited for; matrix products, arithmetic and copies ran while one was open for 0% of the time, Pallas kernels for 0%

profile of v1, /device:TPU:1, one launch (start us, length us, event | category | flops | bytes accessed | tf_op | source)
XLA Modules:
  0.0 658.7 jit_solution(13051394845209485029)
XLA Ops:
  6.5 5.2 stack.12
  11.7 13.9 %all-to-all-start = ((bf16[64,32,2048]{2,1,0:T(8,128)(2,1)}), bf16[64,32,2048]{2,1,0:T(8,128)(2,1)}, u32[]{:S(2)}, u32[]{:S(2)}) async-start(bf16[64,32,2048]{2,1,0:T(8,128)(2,1)} %stack.12), calls=%async_computation | async-start | bytes 16777216 | tf_op jit(solution)/shard_map/all_to_all | solution.py:74
  25.7 181.0 %all-to-all-done = bf16[64,32,2048]{2,1,0:T(8,128)(2,1)} async-done(((bf16[64,32,2048]{2,1,0:T(8,128)(2,1)}), bf16[64,32,2048]{2,1,0:T(8,128)(2,1)}, u32[]{:S(2)}, u32[]{:S(2)}) %all-to-all-start) | async-done | bytes 8388640 | tf_op jit(solution)/shard_map/all_to_all | solution.py:74
  206.7 4.4 bitcast_reduce_fusion
  211.1 4.0 bitcast_reduce_fusion.1
  215.1 4.0 bitcast_reduce_fusion.2
  219.1 7.2 %bitcast_reduce_fusion.3 = (f32[2048,8]{0,1:T(8,128)S(1)}, f32[2048,1024]{0,1:T(8,128)}) fusion(bf16[1024,2048]{1,0:T(8,128)(2,1)S(1)} %copy-done.1, bf16[2048,2048]{1,0:T(8,128)(2,1)} %bitcast.1), kind=kOutput, calls=%fused_computation.23 | convolution fusion | flops 2151661568 | bytes 11599872 | tf_op jit(solution)/shard_map/qs,rs->qr/dot_general | solution.py:45
  226.3 4.8 fusion.15
  231.3 1.5 fusion.9
  232.8 1.7 fusion.11
  234.5 1.5 fusion.13
  237.4 289.2 %all-gather.3.cloned.1.call-done = f32[256,8,2048]{2,1,0:T(8,128)} async-done(((f32[4,8,2048]{2,1,0:T(8,128)}), f32[256,8,2048]{2,1,0:T(8,128)}) %all-gather.3.cloned.1.call-update) | async-done | bytes 16777232 | tf_op jit(solution)/shard_map/all_gather | solution.py:14
  527.6 76.0 %while.15 = (s32[]{:T(128)}, f32[4,8,2048]{2,1,0:T(8,128)S(1)}, f32[64,4,8,2048]{3,2,1,0:T(8,128)}, s32[]{:T(128)}, s32[]{:T(128)}, /*index=5*/s32[]{:T(128)}) while((s32[]{:T(128)}, f32[4,8,2048]{2,1,0:T(8,128)S(1)}, f32[64,4,8,2048]{3,2,1,0:T(8,128)}, s32[]{:T(128)}, s32[]{:T(128)}, /*index=5*/s32[]{:T(128)}) %tuple.60), condition=%wide.region_17.18_spmd, body=%wide.region_16.17_spmd.sunk | while | flops 327685 | bytes 786539 | solution.py:20
  527.6 1.2 fusion.53
  528.8 1.2 fusion.53
  530.0 1.2 fusion.53
  531.2 1.2 fusion.53
  532.4 1.2 fusion.53
  533.6 1.2 fusion.53
  534.8 1.2 fusion.53
  536.0 1.2 fusion.53
  537.2 1.2 fusion.53
  538.4 1.2 fusion.53
  539.6 1.2 fusion.53
  540.9 1.2 fusion.53
  542.1 1.2 fusion.53
  543.3 1.2 fusion.53
  544.5 1.2 fusion.53
  545.7 1.2 fusion.53
  546.9 1.2 fusion.53
  548.1 1.2 fusion.53
  549.3 1.2 fusion.53
  550.5 1.2 fusion.53
  551.7 1.2 fusion.53
  552.9 1.2 fusion.53
  554.1 1.2 fusion.53
  555.3 1.2 fusion.53
  556.5 1.2 fusion.53
  557.7 1.2 fusion.53
  558.9 1.2 fusion.53
  560.1 1.2 fusion.53
  561.3 1.2 fusion.53
  562.6 1.2 fusion.53
  563.8 1.2 fusion.53
  565.0 1.2 fusion.53
  566.2 1.2 fusion.53
  567.4 1.2 fusion.53
  568.6 1.2 fusion.53
  569.8 1.2 fusion.53
  571.0 1.2 fusion.53
  573.4 1.2 fusion.53
  575.8 1.2 fusion.53
  578.2 1.2 fusion.53
  580.6 1.2 fusion.53
  583.1 1.2 fusion.53
  585.5 1.2 fusion.53
  587.9 1.2 fusion.53
  590.3 1.2 fusion.53
  593.9 1.2 fusion.53
  596.3 1.2 fusion.53
  598.7 1.2 fusion.53
  601.1 1.2 fusion.53
  603.7 42.3 %collective-permute-start.1 = (f32[4,8,32]{2,1,0:T(8,128)S(1)}, f32[4,8,32]{2,1,0:T(8,128)S(1)}, u32[]{:S(2)}, u32[]{:S(2)}) collective-permute-start(f32[4,8,32]{2,1,0:T(8,128)S(1)} %dynamic-slice_subtract_fusion), channel_id=1, source_target_pairs={{1,0},{2,1},{3,2},{5,4},{6,5},{7,6},{9,8},{10,9},{11,10},{13,12},{... | collective-permute-start | bytes 12296 | tf_op jit(solution)/shard_map/ppermute | solution.py:31
  646.0 4.3 collective-permute-start
  (40 shorter events, 21.0 us)
Async XLA Ops:
  11.7 13.9 %copy-start.2 = (s32[8]{0:T(128)S(1)}, s32[8]{0:T(128)}, u32[]{:S(2)}) copy-start(s32[8]{0:T(128)} %param.9) | copy-start | bytes 100
  11.7 195.0 %all-to-all-start = ((bf16[64,32,2048]{2,1,0:T(8,128)(2,1)}), bf16[64,32,2048]{2,1,0:T(8,128)(2,1)}, u32[]{:S(2)}, u32[]{:S(2)}) async-start(bf16[64,32,2048]{2,1,0:T(8,128)(2,1)} %stack.12), calls=%async_computation | async-start | bytes 16777216 | tf_op jit(solution)/shard_map/all_to_all | solution.py:74
  25.6 501.0 %all-gather.3.cloned.1.call-start = ((), (), s32[]{:S(2)}) async-start(), calls=%async_computation.1 | async-start | bytes 17039360 | tf_op jit(solution)/shard_map/all_gather | solution.py:14
  206.7 4.4 copy-start.1
  234.5 415.9 %copy-start = (f32[9,8]{0,1:T(8,128)S(1)}, f32[9,8]{0,1:T(8,128)}, u32[]{:S(2)}) copy-start(f32[9,8]{0,1:T(8,128)} %param.10) | copy-start | bytes 868
  234.5 416.7 %copy-start.3 = (f32[8]{0:T(128)S(1)}, f32[8]{0:T(128)}, u32[]{:S(2)}) copy-start(f32[8]{0:T(128)} %param.11) | copy-start | bytes 100
  603.7 46.9 %collective-permute-start.1 = (f32[4,8,32]{2,1,0:T(8,128)S(1)}, f32[4,8,32]{2,1,0:T(8,128)S(1)}, u32[]{:S(2)}, u32[]{:S(2)}) collective-permute-start(f32[4,8,32]{2,1,0:T(8,128)S(1)} %dynamic-slice_subtract_fusion), channel_id=1, source_target_pairs={{1,0},{2,1},{3,2},{5,4},{6,5},{7,6},{9,8},{10,9},{11,10},{13,12},{... | collective-permute-start | bytes 12296 | tf_op jit(solution)/shard_map/ppermute | solution.py:31
  646.0 5.2 collective-permute-start
Sparse Core Ops, SparseCore 0:
  237.6 288.9 all-gather.2
